TPU v7x, 256 devices: a whole 4x4x8 slice. The times are simulated.
256 devices in a mesh: patch: 64 (over z, y, core), mp: 4 (over x).
Axes of the slice: x: 4, y: 4, z: 8, core: 2. Of those that a mesh axis runs over, the one named last changes fastest.
Arguments:
- grid_latent: bfloat16 [65536, 512], P('patch'), may hold values from -6 to 6
- mesh_latent: bfloat16 [8192, 512], P('patch', 'mp'), may hold values from -6 to 6
- edge_weight: bfloat16 [768, 128, 128], P('patch'), may hold values from -0.15625 to 0.15625
- block_source: int32 [768], P('patch'), may hold values from 0 to 511, as said below
- block_live: int32 [768], P('patch'), may hold values from 0 to 1
- mlp_first: bfloat16 [512, 512], replicated, may hold values from -0.25 to 0.25
- mlp_second: bfloat16 [512, 512], P(None, 'mp'), may hold values from -0.25 to 0.25
- mesh_cotangent: bfloat16 [8192, 512], P('patch', 'mp'), may hold values from -6 to 6
Outputs:
- mesh_out: bfloat16 [8192, 512], P('patch', 'mp')
- grad_first: float32 [512, 512], P(None, 'mp')
- grad_second: float32 [512, 512], P(None, 'mp')
Inputs may be any that keep to these rules, and one draw needn't show every extreme that they name: `block_source`: grid patch g lies on the device of index g // 8 along patch, and slot b on the device of index b // 12. On every device at most 1 slots take their source from one device, and some device supplies exactly 1 slots to some device.
All inputs are finite; a program needn't handle non-finite values.
Results may differ from a plain program's by a relative error of at most 0.0058.
Values may be sent and summed in bfloat16 or wider, within the bound.
A program may use at most 64 MiB of HBM per device.

v0:
```python
import functools
import math
import jax
import jax.numpy as jnp
from jax import lax
from jax.sharding import Mesh
from jax.sharding import PartitionSpec as P

PATCH = 128
GPD = 8
BPM = 12
MPD = 1
EBD = 12
PATCH_AXES = ("patch_0", "patch_1", "patch_2")


def joined_along(parts, dim):
    parts = jnp.moveaxis(parts, 0, dim)
    lengths = parts.shape
    return parts.reshape(*lengths[:dim], lengths[dim] * lengths[dim + 1], *lengths[dim + 2 :])


def one_gather(arrays, axis, dims):
    flat = jnp.concatenate([a.reshape(-1) for a in arrays])
    lines, at, finished = (lax.all_gather(flat, axis), 0, [])
    for a, dim in zip(arrays, dims):
        parts = lines[:, at : at + a.size].reshape(-1, *a.shape)
        finished.append(joined_along(parts, dim))
        at += a.size
    return tuple(finished)


def one_axis_at_a_time(array, axes):
    return functools.reduce(lax.psum, axes, array)


def silu_slope(values):
    sigmoid = jax.nn.sigmoid(values)
    return sigmoid * (1.0 + values * (1.0 - sigmoid))


def per_device(
    grid_latent,
    mesh_latent,
    edge_weight,
    block_source,
    block_live,
    mlp_first,
    mlp_second,
    mesh_cotangent,
):
    devices = lax.axis_size(PATCH_AXES)
    own_index = lax.axis_index(PATCH_AXES)
    column_index = lax.axis_index("mp")
    grid_rows = grid_latent.shape[0]
    width_local = mlp_second.shape[1]
    hidden_local = mlp_first.shape[1] // lax.axis_size("mp")
    block_width = PATCH * width_local
    slot_cap = (EBD + devices - 1) // devices
    pre_act = jnp.dot(grid_latent, mlp_first, preferred_element_type=jnp.float32)
    hidden = jax.nn.silu(pre_act).astype(jnp.bfloat16)
    message = jnp.dot(hidden, mlp_second, preferred_element_type=jnp.float32).astype(jnp.bfloat16)
    message_flat = message.reshape(GPD, block_width)
    live_local = block_live.astype(jnp.float32)[:, None, None]
    every_source, every_live = one_gather((block_source, block_live), PATCH_AXES, (0, 0))
    every_source = every_source.reshape(devices, EBD)
    every_live = every_live.reshape(devices, EBD)
    source_device = every_source // GPD
    source_patch = every_source % GPD
    slot_order = jnp.arange(EBD)
    same_source = (source_device[:, :, None] == source_device[:, None, :]) & (
        slot_order[None, None, :] < slot_order[None, :, None]
    )
    slot_rank = jnp.sum(same_source, axis=2)
    own_sources = source_device[own_index]
    own_ranks = slot_rank[own_index]
    wanted = (source_device == own_index) & (every_live == 1)
    matches = (
        wanted[:, :, None, None]
        & (slot_rank[:, :, None, None] == jnp.arange(slot_cap)[None, None, :, None])
        & (source_patch[:, :, None, None] == jnp.arange(GPD)[None, None, None, :])
    )
    picking = jnp.sum(matches, axis=1).reshape(devices * slot_cap, GPD).astype(jnp.bfloat16)
    outgoing = (
        jnp.dot(picking, message_flat, preferred_element_type=jnp.float32)
        .astype(jnp.bfloat16)
        .reshape(devices, slot_cap, block_width)
    )
    incoming = lax.all_to_all(
        outgoing, PATCH_AXES, split_axis=0, concat_axis=0, tiled=True
    ).reshape(devices * slot_cap, block_width)
    lookup = own_sources * slot_cap + own_ranks
    block_input = jnp.take(incoming, lookup, axis=0).reshape(EBD, PATCH, width_local)
    products = (
        jnp.einsum("bpq,bqc->bpc", edge_weight, block_input, preferred_element_type=jnp.float32)
        * live_local
    )
    summed = (
        products.reshape(MPD, BPM, PATCH, width_local).sum(axis=1).reshape(MPD * PATCH, width_local)
    )
    mesh_out = (mesh_latent.astype(jnp.float32) + summed).astype(jnp.bfloat16)
    cotangent_blocks = jnp.broadcast_to(
        mesh_cotangent.reshape(MPD, 1, PATCH, width_local), (MPD, BPM, PATCH, width_local)
    ).reshape(EBD, PATCH, width_local)
    adjoint = (
        jnp.einsum(
            "bqp,bqc->bpc", edge_weight, cotangent_blocks, preferred_element_type=jnp.float32
        )
        * live_local
    ).astype(jnp.bfloat16)
    adjoint = adjoint.reshape(EBD, block_width)
    slot_rows = devices * slot_cap
    scatter_table = (
        (jnp.arange(slot_rows)[:, None] == lookup[None, :]) & (block_live[None, :] == 1)
    ).astype(jnp.bfloat16)
    returning = jnp.dot(scatter_table, adjoint, preferred_element_type=jnp.float32).astype(
        jnp.bfloat16
    )
    back_flat = lax.all_to_all(
        returning.reshape(devices, slot_cap, block_width),
        PATCH_AXES,
        split_axis=0,
        concat_axis=0,
        tiled=True,
    ).reshape(devices * slot_cap, block_width)
    grad_message = lax.dot_general(
        picking, back_flat, (((0,), (0,)), ((), ())), preferred_element_type=jnp.float32
    )
    grad_message = grad_message.astype(jnp.bfloat16).reshape(grid_rows, width_local)
    scaling = 1.0 / math.sqrt(grid_rows * devices)
    grad_second = (
        lax.dot_general(
            hidden, grad_message, (((0,), (0,)), ((), ())), preferred_element_type=jnp.float32
        )
        * scaling
    )
    grad_piece = lax.all_gather(grad_message, "mp", axis=1, tiled=True)
    second_piece = lax.all_gather(mlp_second, "mp", axis=1, tiled=True)
    rows_of_second = lax.dynamic_slice_in_dim(
        second_piece, column_index * hidden_local, hidden_local, 0
    )
    grad_hidden = lax.dot_general(
        rows_of_second, grad_piece, (((1,), (1,)), ((), ())), preferred_element_type=jnp.float32
    )
    pre_slice = lax.dynamic_slice_in_dim(pre_act, column_index * hidden_local, hidden_local, 1).T
    grad_pre = (grad_hidden * silu_slope(pre_slice)).astype(jnp.bfloat16)
    grad_first = (
        lax.dot_general(
            grid_latent, grad_pre, (((0,), (1,)), ((), ())), preferred_element_type=jnp.float32
        )
        * scaling
    )
    grad_first, grad_second = (
        one_axis_at_a_time(grad_first, PATCH_AXES),
        one_axis_at_a_time(grad_second, PATCH_AXES),
    )
    return (mesh_out, grad_first, grad_second)


def solution(mesh):
    torus = Mesh(
        mesh.devices.reshape(8, 4, 2, mesh.shape["mp"]), ("patch_0", "patch_1", "patch_2", "mp")
    )
    in_specs = (
        P(PATCH_AXES, None),
        P(PATCH_AXES, "mp"),
        P(PATCH_AXES, None, None),
        P(PATCH_AXES),
        P(PATCH_AXES),
        P(),
        P(None, "mp"),
        P(PATCH_AXES, "mp"),
    )
    out_specs = (P(PATCH_AXES, "mp"), P(None, "mp"), P(None, "mp"))
    return jax.shard_map(
        per_device, mesh=torus, in_specs=in_specs, out_specs=out_specs, check_vma=False
    )
```

profile of v0, /device:TPU:1, one launch (start us, length us, event | category | flops | bytes accessed | tf_op | source)
XLA Modules:
  0.0 328.0 jit_solution(325961317000444766)
XLA Ops:
  11.4 21.0 %all-reduce = s32[1536]{0:T(1024)S(1)} all-reduce(s32[1536]{0:T(1024)S(1)} %add_dynamic-update-slice_fusion), channel_id=2, replica_groups=mesh['patch_0'=8,'patch_1'=4,'patch_2'=2,'mp'=4] {'patch_0','patch_1','p..., use_global_device_ids=true, to_apply=%add | all-reduce | flops 1536 | bytes 12288
  36.1 1.7 fusion.1
  38.4 2.9 reduce.8
  41.2 4.5 %reshape.158 = bf16[64,2,8192]{2,1,0:T(2,128)(2,1)} reshape(bf16[64,16384]{1,0:T(8,128)(2,1)} %reduce.8) | data formatting | bytes 4194304
  45.7 8.9 %all-to-all-start.1 = ((bf16[64,2,8192]{2,1,0:T(2,128)(2,1)}), bf16[64,2,8192]{2,1,0:T(2,128)(2,1)S(1)}, u32[]{:S(2)}, u32[]{:S(2)}) async-start(bf16[64,2,8192]{2,1,0:T(2,128)(2,1)} %reshape.158), calls=%async_computation.1 | async-start | bytes 4194304 | tf_op jit(solution)/shard_map/all_to_all | solution.py:119
  55.3 3.3 %multiply_convert_fusion = (bf16[1024,512]{1,0:T(8,128)(2,1)S(1)}, f32[1024,512]{1,0:T(8,128)}) fusion(bf16[1024,512]{1,0:T(8,128)(2,1)S(1)} %copy-done, bf16[512,512]{1,0:T(8,128)(2,1)} %param.13), kind=kOutput, calls=%fused_computation.9 | convolution fusion | flops 539492352 | bytes 4718592 | tf_op jit(solution)/shard_map/dot_general | solution.py:60
  63.2 2.1 fusion
  65.3 4.5 %reduce.7 = bf16[64,16384]{1,0:T(8,128)(2,1)} reduce(bf16[64,1,16384]{2,0,1:T(8,128)(2,1)} %fusion, bf16[]{:T(256)} %broadcast.136), dimensions={1}, to_apply=%copy.46.reduce_sub_computation | reduce | bytes 4194306 | tf_op jit(solution)/shard_map/reshape | solution.py:87
  69.8 4.5 %reshape.156 = bf16[64,2,8192]{2,1,0:T(2,128)(2,1)} reshape(bf16[64,16384]{1,0:T(8,128)(2,1)} %reduce.7) | data formatting | bytes 4194304
  74.3 30.3 %all-to-all-done.1 = bf16[64,2,8192]{2,1,0:T(2,128)(2,1)S(1)} async-done(((bf16[64,2,8192]{2,1,0:T(2,128)(2,1)}), bf16[64,2,8192]{2,1,0:T(2,128)(2,1)S(1)}, u32[]{:S(2)}, u32[]{:S(2)}) %all-to-all-start.1) | async-done | bytes 2097184 | tf_op jit(solution)/shard_map/all_to_all | solution.py:119
  106.0 6.8 %all-to-all-start = ((bf16[64,2,8192]{2,1,0:T(2,128)(2,1)}), bf16[64,2,8192]{2,1,0:T(2,128)(2,1)S(1)}, u32[]{:S(2)}, u32[]{:S(2)}) async-start(bf16[64,2,8192]{2,1,0:T(2,128)(2,1)} %reshape.156), calls=%async_computation | async-start | bytes 4194304 | tf_op jit(solution)/shard_map/all_to_all | solution.py:89
  112.8 10.4 %reshape.159 = bf16[64,1,16384]{2,1,0:T(2,128)(2,1)} reshape(bf16[64,2,8192]{2,1,0:T(2,128)(2,1)} %copy-done.1) | data formatting | bytes 4194304
  123.2 4.5 %convolution_convert_fusion.2 = bf16[8,16384]{1,0:T(8,128)(2,1)S(1)} fusion(bf16[64,1,16384]{2,1,0:T(2,128)(2,1)} %reshape.159, s32[64,8]{0,1:T(8,128)S(1)} %convert_reduce_fusion.1), kind=kOutput, calls=%fused_computation.5 | convolution fusion | flops 16908800 | bytes 2361344 | tf_op jit(solution)/shard_map/dot_general | solution.py:126
  128.6 12.8 %all_gather.14 = bf16[512,512]{1,0:T(8,128)(2,1)} all-gather(bf16[512,128]{1,0:T(8,128)(2,1)S(1)} %copy-done.3), channel_id=1, replica_groups=mesh['patch_0'=8,'patch_1'=4,'patch_2'=2,'mp'=4] {'mp'}, dimensions={1}, use_global_device_ids=true | all-gather | bytes 655360 | tf_op jit(solution)/shard_map/all_gather | solution.py:138
  141.3 2.5 convolution_multiply_fusion.3
  143.8 12.4 %all-gather.3.cloned.1.call-done = bf16[1024,512]{1,0:T(8,128)(2,1)} async-done(((bf16[1024,128]{1,0:T(8,128)(2,1)}), bf16[1024,512]{1,0:T(8,128)(2,1)}) %all-gather.3.cloned.1.call-update) | async-done | bytes 1048592 | tf_op jit(solution)/shard_map/all_gather | solution.py:137
  156.3 2.9 fusion.9
  159.2 71.2 %all-reduce.8.cloned.1.call-done = (f32[512,128]{0,1:T(8,128)}, f32[512,128]{1,0:T(8,128)}) async-done(((f32[512,128]{0,1:T(8,128)}, f32[512,128]{1,0:T(8,128)}), (f32[512,128]{0,1:T(8,128)}, f32[512,128]{1,0:T(8,128)})) %all-reduce.8.cloned.1.call-update) | async-done | bytes 524304 | tf_op jit(solution)/shard_map/psum | solution.py:34
  230.6 51.8 %all-reduce.10.cloned.1.call-done = (f32[512,128]{0,1:T(8,128)}, f32[512,128]{1,0:T(8,128)}) async-done(((f32[512,128]{0,1:T(8,128)}, f32[512,128]{1,0:T(8,128)}), (f32[512,128]{0,1:T(8,128)}, f32[512,128]{1,0:T(8,128)})) %all-reduce.10.cloned.1.call-update) | async-done | bytes 524304 | tf_op jit(solution)/shard_map/psum | solution.py:34
  282.6 6.7 %reshape.157 = bf16[64,1,16384]{2,1,0:T(2,128)(2,1)} reshape(bf16[64,2,8192]{2,1,0:T(2,128)(2,1)S(1)} %all-to-all-done) | data formatting | bytes 4194304
  289.3 4.5 %copy.66 = bf16[64,1,16384]{2,0,1:T(8,128)(2,1)S(1)} copy(bf16[64,1,16384]{2,1,0:T(2,128)(2,1)} %reshape.157) | data formatting | bytes 4194304
  298.0 20.0 %all-reduce.12.cloned.1.call-done = (f32[512,128]{0,1:T(8,128)}, f32[512,128]{1,0:T(8,128)}) async-done(((f32[512,128]{0,1:T(8,128)}, f32[512,128]{1,0:T(8,128)}), (f32[512,128]{0,1:T(8,128)}, f32[512,128]{1,0:T(8,128)})) %all-reduce.12.cloned.1.call-update) | async-done | bytes 524304 | tf_op jit(solution)/shard_map/psum | solution.py:34
  318.0 1.8 copy.52
  319.8 1.7 copy.76
  (62 shorter events, 19.8 us)
Async XLA Ops:
  7.2 48.1 %copy-start = (bf16[1024,512]{1,0:T(8,128)(2,1)S(1)}, bf16[1024,512]{1,0:T(8,128)(2,1)}, u32[]{:S(2)}) copy-start(bf16[1024,512]{1,0:T(8,128)(2,1)} %param.8) | copy-start | bytes 3145732
  7.9 29.8 %copy-start.8 = (f32[12]{0:T(128)}, f32[12]{0:T(128)S(1)}, u32[]{:S(2)}) copy-start(f32[12]{0:T(128)S(1)} %convert_element_type.60) | copy-start | bytes 148
  36.1 5.2 %copy-start.6 = (s32[12]{0:T(128)}, s32[12]{0:T(128)S(1)}, u32[]{:S(2)}) copy-start(s32[12]{0:T(128)S(1)} %add_reduce_fusion) | copy-start | bytes 148
  45.7 58.9 %all-to-all-start.1 = ((bf16[64,2,8192]{2,1,0:T(2,128)(2,1)}), bf16[64,2,8192]{2,1,0:T(2,128)(2,1)S(1)}, u32[]{:S(2)}, u32[]{:S(2)}) async-start(bf16[64,2,8192]{2,1,0:T(2,128)(2,1)} %reshape.158), calls=%async_computation.1 | async-start | bytes 4194304 | tf_op jit(solution)/shard_map/all_to_all | solution.py:119
  55.3 4.3 %copy-start.3 = (bf16[512,128]{1,0:T(8,128)(2,1)S(1)}, bf16[512,128]{1,0:T(8,128)(2,1)}, u32[]{:S(2)}) copy-start(bf16[512,128]{1,0:T(8,128)(2,1)} %param.14) | copy-start | bytes 393220
  58.6 1.0 copy-start.2
  104.6 1.4 copy-start.1
  106.0 176.6 %all-to-all-start = ((bf16[64,2,8192]{2,1,0:T(2,128)(2,1)}), bf16[64,2,8192]{2,1,0:T(2,128)(2,1)S(1)}, u32[]{:S(2)}, u32[]{:S(2)}) async-start(bf16[64,2,8192]{2,1,0:T(2,128)(2,1)} %reshape.156), calls=%async_computation | async-start | bytes 4194304 | tf_op jit(solution)/shard_map/all_to_all | solution.py:89
  112.8 43.5 %all-gather.3.cloned.1.call-start = ((), (), s32[]{:S(2)}) async-start(), calls=%async_computation.2 | async-start | bytes 1310720 | tf_op jit(solution)/shard_map/all_gather | solution.py:137
  128.5 101.9 %all-reduce.8.cloned.1.call-start = ((), (), s32[]{:S(2)}) async-start(), calls=%async_computation.3 | async-start | bytes 1048576 | tf_op jit(solution)/shard_map/psum | solution.py:34
  156.3 74.3 %copy-start.7 = (s32[12]{0:T(128)S(1)}, s32[12]{0:T(128)}, u32[]{:S(2)}) copy-start(s32[12]{0:T(128)} %copy-done.6) | copy-start | bytes 148
  156.3 126.2 %copy-start.5 = (bf16[128,128]{1,0:T(8,128)(2,1)S(1)}, bf16[128,128]{1,0:T(8,128)(2,1)}, u32[]{:S(2)}) copy-start(bf16[128,128]{1,0:T(8,128)(2,1)} %param.9) | copy-start | bytes 98308
  159.2 123.2 %all-reduce.10.cloned.1.call-start = ((), (), s32[]{:S(2)}) async-start(), calls=%async_computation.4 | async-start | bytes 1048576 | tf_op jit(solution)/shard_map/psum | solution.py:34
  230.5 87.5 %all-reduce.12.cloned.1.call-start = ((), (), s32[]{:S(2)}) async-start(), calls=%async_computation.5 | async-start | bytes 1048576 | tf_op jit(solution)/shard_map/psum | solution.py:34
  295.3 1.5 copy-start.4
  295.3 1.5 copy-start.9
Sparse Core Ops, SparseCore 0:
  128.7 27.5 all-gather.2
  159.3 71.1 all-reduce.7
  232.9 49.4 all-reduce.9
  284.9 33.0 all-reduce.11
where the time goes:
time: 329 us; the launch traced here: 328 us
  waiting for transfers between devices  186 us (57%)
  local copies, waits for them, and re-layouts  46 us (14%)
  blocking collectives  33.7 us (10%)
  matrix products  19.9 us (6%)
  starting transfers between devices  15.8 us (5%)
  between operations  14.6 us (4%)
  other arithmetic  12 us (4%)
    psum x3, waiting for transfers between devices, one_axis_at_a_time(): return functools.reduce(lax.psum, axes, array)  143 us
    unnamed x36, local copies, waits for them, and re-layouts  41.5 us
    all_to_all x1, waiting for transfers between devices, per_device(): lax.all_to_all(returning.reshape(devices, slot_cap, block_width), PATCH_A...  30.3 us
    unnamed x1, blocking collectives  21 us
    all_gather x1, blocking collectives, per_device(): second_piece = lax.all_gather(mlp_second, 'mp', axis=1, tiled=True)  12.8 us
    all_gather x1, waiting for transfers between devices, per_device(): grad_piece = lax.all_gather(grad_message, 'mp', axis=1, tiled=True)  12.4 us
    all_to_all x1, starting transfers between devices, per_device(): lax.all_to_all(returning.reshape(devices, slot_cap, block_width), PATCH_A...  8.9 us
    all_to_all x1, starting transfers between devices, per_device(): lax.all_to_all(outgoing, PATCH_AXES, split_axis=0, concat_axis=0, tiled=T...  6.79 us
  transfers between devices with their start and end apart: 6, of which 5 were waited for; matrix products, arithmetic and copies ran while one was open for 17% of the time, Pallas kernels for 0%

commit v1 on v0

--- a/solution.py
+++ b/solution.py
@@ -134,7 +134,9 @@
         )
         * scaling
     )
-    grad_piece = lax.all_gather(grad_message, "mp", axis=1, tiled=True)
+    grad_piece = jnp.concatenate(
+        lax.all_to_all(jnp.stack([grad_message] * lax.axis_size("mp")), "mp", 0, 0), axis=1
+    )
     second_piece = lax.all_gather(mlp_second, "mp", axis=1, tiled=True)
     rows_of_second = lax.dynamic_slice_in_dim(
         second_piece, column_index * hidden_local, hidden_local, 0

time: 329 us -> 335 us (1.018)
  waiting for transfers between devices: 186 us -> 198 us
  starting transfers between devices: 15.8 us -> 21.7 us
  local copies, waits for them, and re-layouts: 46 us -> 40.9 us
  other arithmetic: 12 us -> 8.5 us
    all_to_all x1, waiting for transfers between devices: 30.3 us -> 49.9 us  [per_device(): lax.all_to_all(returning.reshape(devices, slot_cap, block_width), PATCH_A...]
    all_gather x1 -> x0, waiting for transfers between devices: 12.4 us -> none  [per_device(): grad_piece = lax.all_gather(grad_message, 'mp', axis=1, tiled=True)]
    unnamed x36 -> x28, local copies, waits for them, and re-layouts: 41.5 us -> 36.1 us
    psum x3, waiting for transfers between devices: 143 us -> 148 us  [one_axis_at_a_time(): return functools.reduce(lax.psum, axes, array)]
    all_to_all x0 -> x1, starting transfers between devices: none -> 4.26 us  [per_device(): lax.all_to_all(jnp.stack([grad_message] * lax.axis_size('mp')), 'mp', 0, 0)]
  transfers between devices with their start and end apart: 6 -> 6, of which waited for: 5 -> 4; matrix products, arithmetic and copies ran while one was open for 17% -> 10% of each run, Pallas kernels for 0% -> 0%
where the time goes in v1:
time: 335 us; the launch traced here: 334 us
  waiting for transfers between devices  198 us (59%)
  local copies, waits for them, and re-layouts  40.9 us (12%)
  blocking collectives  32.8 us (10%)
  starting transfers between devices  21.7 us (6%)
  matrix products  17.7 us (5%)
  between operations  14.7 us (4%)
  other arithmetic  8.5 us (3%)
    psum x3, waiting for transfers between devices, one_axis_at_a_time(): return functools.reduce(lax.psum, axes, array)  148 us
    all_to_all x1, waiting for transfers between devices, per_device(): lax.all_to_all(returning.reshape(devices, slot_cap, block_width), PATCH_A...  49.9 us
    unnamed x28, local copies, waits for them, and re-layouts  36.1 us
    unnamed x1, blocking collectives  21 us
    all_gather x1, blocking collectives, per_device(): second_piece = lax.all_gather(mlp_second, 'mp', axis=1, tiled=True)  11.8 us
    all_to_all x1, starting transfers between devices, per_device(): lax.all_to_all(returning.reshape(devices, slot_cap, block_width), PATCH_A...  8.91 us
    all_to_all x1, starting transfers between devices, per_device(): lax.all_to_all(outgoing, PATCH_AXES, split_axis=0, concat_axis=0, tiled=T...  8.43 us
  transfers between devices with their start and end apart: 6, of which 4 were waited for; matrix products, arithmetic and copies ran while one was open for 10% of the time, Pallas kernels for 0%

profile of v1, /device:TPU:1, one launch (start us, length us, event | category | flops | bytes accessed | tf_op | source)
XLA Modules:
  0.0 334.2 jit_solution(15725479134546190152)
XLA Ops:
  11.4 21.0 %all-reduce = s32[1536]{0:T(1024)S(1)} all-reduce(s32[1536]{0:T(1024)S(1)} %add_dynamic-update-slice_fusion), channel_id=2, replica_groups=mesh['patch_0'=8,'patch_1'=4,'patch_2'=2,'mp'=4] {'patch_0','patch_1','p..., use_global_device_ids=true, to_apply=%add | all-reduce | flops 1536 | bytes 12288
  35.5 1.7 fusion.1
  37.7 2.9 reduce.8
  40.6 4.5 %reshape.165 = bf16[64,2,8192]{2,1,0:T(2,128)(2,1)} reshape(bf16[64,16384]{1,0:T(8,128)(2,1)} %reduce.8) | data formatting | bytes 4194304
  45.1 8.9 %all-to-all-start.1 = ((bf16[64,2,8192]{2,1,0:T(2,128)(2,1)}), bf16[64,2,8192]{2,1,0:T(2,128)(2,1)S(1)}, u32[]{:S(2)}, u32[]{:S(2)}) async-start(bf16[64,2,8192]{2,1,0:T(2,128)(2,1)} %reshape.165), calls=%async_computation.1 | async-start | bytes 4194304 | tf_op jit(solution)/shard_map/all_to_all | solution.py:119
  54.2 49.9 %all-to-all-done.1 = bf16[64,2,8192]{2,1,0:T(2,128)(2,1)S(1)} async-done(((bf16[64,2,8192]{2,1,0:T(2,128)(2,1)}), bf16[64,2,8192]{2,1,0:T(2,128)(2,1)S(1)}, u32[]{:S(2)}, u32[]{:S(2)}) %all-to-all-start.1) | async-done | bytes 2097184 | tf_op jit(solution)/shard_map/all_to_all | solution.py:119
  104.0 6.8 %reshape.166 = bf16[64,1,16384]{2,1,0:T(2,128)(2,1)} reshape(bf16[64,2,8192]{2,1,0:T(2,128)(2,1)S(1)} %all-to-all-done.1) | data formatting | bytes 4194304
  110.8 4.5 %convolution_convert_fusion.2 = bf16[8,16384]{1,0:T(8,128)(2,1)S(1)} fusion(bf16[64,1,16384]{2,1,0:T(2,128)(2,1)} %reshape.166, s32[64,8]{0,1:T(8,128)S(1)} %convert_reduce_fusion.1), kind=kOutput, calls=%fused_computation.5 | convolution fusion | flops 16908800 | bytes 2361344 | tf_op jit(solution)/shard_map/dot_general | solution.py:126
  116.7 4.3 %all-to-all-start.2 = ((bf16[4,1024,128]{1,2,0:T(8,128)(2,1)}), bf16[4,1024,128]{1,2,0:T(8,128)(2,1)}, u32[]{:S(2)}, u32[]{:S(2)}) async-start(bf16[4,1024,128]{1,2,0:T(8,128)(2,1)} %stack.3), calls=%async_computation.2 | async-start | bytes 2097152 | tf_op jit(solution)/shard_map/all_to_all | solution.py:138
  121.0 2.2 multiply_convert_fusion
  125.5 1.7 fusion
  127.2 2.9 reduce.7
  130.2 4.5 %reshape.163 = bf16[64,2,8192]{2,1,0:T(2,128)(2,1)} reshape(bf16[64,16384]{1,0:T(8,128)(2,1)} %reduce.7) | data formatting | bytes 4194304
  134.6 8.4 %all-to-all-start = ((bf16[64,2,8192]{2,1,0:T(2,128)(2,1)}), bf16[64,2,8192]{2,1,0:T(2,128)(2,1)S(1)}, u32[]{:S(2)}, u32[]{:S(2)}) async-start(bf16[64,2,8192]{2,1,0:T(2,128)(2,1)} %reshape.163), calls=%async_computation | async-start | bytes 4194304 | tf_op jit(solution)/shard_map/all_to_all | solution.py:89
  143.1 11.8 %all_gather.11 = bf16[512,512]{1,0:T(8,128)(2,1)} all-gather(bf16[512,128]{1,0:T(8,128)(2,1)S(1)} %copy-done.2), channel_id=1, replica_groups=mesh['patch_0'=8,'patch_1'=4,'patch_2'=2,'mp'=4] {'mp'}, dimensions={1}, use_global_device_ids=true | all-gather | bytes 655360 | tf_op jit(solution)/shard_map/all_gather | solution.py:140
  154.9 2.4 convolution_multiply_fusion.3
  157.3 3.0 fusion.9
  160.4 76.2 %all-reduce.8.cloned.1.call-done = (f32[512,128]{0,1:T(8,128)}, f32[512,128]{1,0:T(8,128)}) async-done(((f32[512,128]{0,1:T(8,128)}, f32[512,128]{1,0:T(8,128)}), (f32[512,128]{0,1:T(8,128)}, f32[512,128]{1,0:T(8,128)})) %all-reduce.8.cloned.1.call-update) | async-done | bytes 524304 | tf_op jit(solution)/shard_map/psum | solution.py:34
  236.7 51.8 %all-reduce.10.cloned.1.call-done = (f32[512,128]{0,1:T(8,128)}, f32[512,128]{1,0:T(8,128)}) async-done(((f32[512,128]{0,1:T(8,128)}, f32[512,128]{1,0:T(8,128)}), (f32[512,128]{0,1:T(8,128)}, f32[512,128]{1,0:T(8,128)})) %all-reduce.10.cloned.1.call-update) | async-done | bytes 524304 | tf_op jit(solution)/shard_map/psum | solution.py:34
  288.7 6.8 %reshape.164 = bf16[64,1,16384]{2,1,0:T(2,128)(2,1)} reshape(bf16[64,2,8192]{2,1,0:T(2,128)(2,1)S(1)} %all-to-all-done) | data formatting | bytes 4194304
  295.5 4.5 %copy.71 = bf16[64,1,16384]{2,0,1:T(8,128)(2,1)S(1)} copy(bf16[64,1,16384]{2,1,0:T(2,128)(2,1)} %reshape.164) | data formatting | bytes 4194304
  304.2 20.1 %all-reduce.12.cloned.1.call-done = (f32[512,128]{0,1:T(8,128)}, f32[512,128]{1,0:T(8,128)}) async-done(((f32[512,128]{0,1:T(8,128)}, f32[512,128]{1,0:T(8,128)}), (f32[512,128]{0,1:T(8,128)}, f32[512,128]{1,0:T(8,128)})) %all-reduce.12.cloned.1.call-update) | async-done | bytes 524304 | tf_op jit(solution)/shard_map/psum | solution.py:34
  324.2 1.8 copy.57
  326.0 1.7 copy.81
  (55 shorter events, 15.4 us)
Async XLA Ops:
  7.2 113.8 %copy-start = (bf16[1024,512]{1,0:T(8,128)(2,1)S(1)}, bf16[1024,512]{1,0:T(8,128)(2,1)}, u32[]{:S(2)}) copy-start(bf16[1024,512]{1,0:T(8,128)(2,1)} %param.8) | copy-start | bytes 3145732
  45.1 58.9 %all-to-all-start.1 = ((bf16[64,2,8192]{2,1,0:T(2,128)(2,1)}), bf16[64,2,8192]{2,1,0:T(2,128)(2,1)S(1)}, u32[]{:S(2)}, u32[]{:S(2)}) async-start(bf16[64,2,8192]{2,1,0:T(2,128)(2,1)} %reshape.165), calls=%async_computation.1 | async-start | bytes 4194304 | tf_op jit(solution)/shard_map/all_to_all | solution.py:119
  115.3 5.7 %copy-start.5 = (bf16[512,512]{1,0:T(8,128)(2,1)S(1)}, bf16[512,512]{1,0:T(8,128)(2,1)}, u32[]{:S(2)}) copy-start(bf16[512,512]{1,0:T(8,128)(2,1)} %param.13) | copy-start | bytes 1572868
  116.7 17.9 %all-to-all-start.2 = ((bf16[4,1024,128]{1,2,0:T(8,128)(2,1)}), bf16[4,1024,128]{1,2,0:T(8,128)(2,1)}, u32[]{:S(2)}, u32[]{:S(2)}) async-start(bf16[4,1024,128]{1,2,0:T(8,128)(2,1)} %stack.3), calls=%async_computation.2 | async-start | bytes 2097152 | tf_op jit(solution)/shard_map/all_to_all | solution.py:138
  121.0 3.3 copy-start.2
  123.2 1.1 copy-start.1
  134.6 154.0 %all-to-all-start = ((bf16[64,2,8192]{2,1,0:T(2,128)(2,1)}), bf16[64,2,8192]{2,1,0:T(2,128)(2,1)S(1)}, u32[]{:S(2)}, u32[]{:S(2)}) async-start(bf16[64,2,8192]{2,1,0:T(2,128)(2,1)} %reshape.163), calls=%async_computation | async-start | bytes 4194304 | tf_op jit(solution)/shard_map/all_to_all | solution.py:89
  143.1 93.5 %all-reduce.8.cloned.1.call-start = ((), (), s32[]{:S(2)}) async-start(), calls=%async_computation.3 | async-start | bytes 1048576 | tf_op jit(solution)/shard_map/psum | solution.py:34
  157.3 131.2 %copy-start.4 = (bf16[128,128]{1,0:T(8,128)(2,1)S(1)}, bf16[128,128]{1,0:T(8,128)(2,1)}, u32[]{:S(2)}) copy-start(bf16[128,128]{1,0:T(8,128)(2,1)} %param.9) | copy-start | bytes 98308
  160.3 128.2 %all-reduce.10.cloned.1.call-start = ((), (), s32[]{:S(2)}) async-start(), calls=%async_computation.4 | async-start | bytes 1048576 | tf_op jit(solution)/shard_map/psum | solution.py:34
  236.6 87.6 %all-reduce.12.cloned.1.call-start = ((), (), s32[]{:S(2)}) async-start(), calls=%async_computation.5 | async-start | bytes 1048576 | tf_op jit(solution)/shard_map/psum | solution.py:34
  301.5 1.5 copy-start.3
Sparse Core Ops, SparseCore 0:
  160.4 76.0 all-reduce.7
  239.0 49.4 all-reduce.9
  291.1 33.0 all-reduce.11
